TPU v7x, 32 devices: a whole 2x2x4 slice. The times are simulated.
32 devices in a mesh: groups: 2 (over x), tile: 16 (over z, y, core).
Axes of the slice: x: 2, y: 2, z: 4, core: 2. Of those that a mesh axis runs over, the one named last changes fastest.
Arguments:
- video_latent: bfloat16 [96, 160, 384], P(('groups', 'tile')), parts along dimension 0, may hold values from -6 to 6
- conv_cache: bfloat16 [96, 160, 384], P(('groups', 'tile')), parts along dimension 0, may hold values from -6 to 6
- norm_gain: float32 [384], replicated, may hold values from 0.1 to 1.9
- conv_kernel: bfloat16 [3, 3, 3, 384, 384], replicated, may hold values from -0.0625 to 0.0625
- attend_gain: float32 [384], replicated, may hold values from 0.1 to 1.9
- w_query: bfloat16 [384, 384], replicated, may hold values from -2 to 6
- w_key: bfloat16 [384, 384], replicated, may hold values from -2 to 6
- w_value: bfloat16 [384, 384], replicated, may hold values from -0.3125 to 0.3125
- w_output: bfloat16 [384, 384], replicated, may hold values from -0.3125 to 0.3125
Outputs:
- result: bfloat16 [96, 160, 384], P(('groups', 'tile')), parts along dimension 0
There are 2 independent parts, one for each index of `groups`. A program takes and returns all parts, laid end to end along the dimension named above; an argument that names none is the same for every part. Nothing has to cross between parts.
All inputs are finite; a program needn't handle non-finite values.
Results may differ from a plain program's by a relative error of at most 0.007.
Values may be sent and summed in bfloat16 or wider, within the bound.
No kernel may reach another device: no remote copies, remote signals or barrier semaphores. Data moves between devices by JAX's collectives and lax.ppermute only.
A program may use at most 64 MiB of HBM per device.

v0:
```python
import jax
import jax.numpy as jnp
from jax import lax
from jax.sharding import PartitionSpec as P


def from_behind(value, axis, steps):
    count = lax.axis_size(axis)
    pairs = [(source, (source + steps) % count) for source in range(count)]
    return lax.ppermute(value, axis, pairs)


def passed_along(block, axis, distance):
    devices = range(lax.axis_size(axis))
    route = [(i - distance, i) for i in devices if i - distance in devices]
    return lax.ppermute(block, axis, route)


def swapped(value, axis, bit):
    mask = 2**bit
    pairs = [(source, source ^ mask) for source in range(lax.axis_size(axis))]
    return lax.ppermute(value, axis, pairs)


def rms_scale(inputs, scale_gain):
    floats = inputs.astype(jnp.float32)
    return (
        floats * lax.rsqrt(jnp.mean(floats * floats, axis=-1, keepdims=True) + 1e-06) * scale_gain
    )


def body(
    video_latent, conv_cache, norm_gain, conv_kernel, attend_gain, w_query, w_key, w_value, w_output
):
    rows_local, cols_all, channels = video_latent.shape
    tiles = lax.axis_size("tile")
    row_tiles = min(16, tiles // 2)
    row_bits = row_tiles.bit_length() - 1
    frames = tiles // row_tiles
    frame_bits = frames.bit_length() - 1
    position = lax.axis_index("tile")
    time_group = position % frames
    activated = jax.nn.silu(rms_scale(video_latent, norm_gain)).astype(jnp.bfloat16)
    frame_pair = jnp.stack([activated, conv_cache])
    before_one = from_behind(frame_pair, "tile", 1)
    before_two = from_behind(before_one, "tile", 1)
    frame_one = jnp.where(time_group >= 1, before_one[0], before_one[1])
    frame_two = jnp.where(time_group >= 2, before_two[0], before_two[1])
    stacked = jnp.stack([frame_two, frame_one, frame_pair[0]])
    rim_above = passed_along(stacked[:, -1:], "tile", frames)
    rim_below = passed_along(stacked[:, :1], "tile", -frames)
    stacked = jnp.concatenate([rim_above, stacked, rim_below], axis=1)
    padded = jnp.pad(stacked, ((0, 0), (0, 0), (1, 1), (0, 0)))
    summed = jnp.zeros((rows_local * cols_all, channels), jnp.float32)
    for time_tap in range(3):
        for row_tap in range(3):
            for col_tap in range(3):
                window = padded[
                    time_tap, row_tap : row_tap + rows_local, col_tap : col_tap + cols_all
                ]
                summed = summed + jnp.dot(
                    window.reshape(-1, channels),
                    conv_kernel[time_tap, row_tap, col_tap],
                    preferred_element_type=jnp.float32,
                )
    residual = (video_latent.astype(jnp.float32) + summed.reshape(video_latent.shape)).astype(
        jnp.bfloat16
    )
    normed = rms_scale(residual, attend_gain).astype(jnp.bfloat16)
    flat_rows = normed.reshape(-1, channels)
    positions = rows_local * cols_all
    queries = jnp.dot(flat_rows, w_query, preferred_element_type=jnp.float32).astype(jnp.bfloat16)
    score_scale = float(channels) ** (-0.5)
    initial = (
        jnp.full((positions,), -1e30, jnp.float32),
        jnp.zeros((positions,), jnp.float32),
        jnp.zeros((positions, channels), jnp.float32),
    )

    def absorb(running, key_part, value_part):
        highest, weight_sum, numerator = running
        scores = (
            jnp.einsum("qc,kc->qk", queries, key_part, preferred_element_type=jnp.float32)
            * score_scale
        )
        new_highest = jnp.maximum(highest, jnp.max(scores, axis=-1))
        rescale = jnp.exp(highest - new_highest)
        weights = jnp.exp(scores - new_highest[:, None])
        weight_sum = weight_sum * rescale + jnp.sum(weights, axis=-1)
        numerator = numerator * rescale[:, None] + jnp.dot(
            weights.astype(jnp.bfloat16), value_part, preferred_element_type=jnp.float32
        )
        return (new_highest, weight_sum, numerator)

    def project_pair(block_rows):
        key_part = jnp.dot(block_rows, w_key, preferred_element_type=jnp.float32).astype(
            jnp.bfloat16
        )
        value_part = jnp.dot(block_rows, w_value, preferred_element_type=jnp.float32).astype(
            jnp.bfloat16
        )
        return (key_part, value_part)

    keys_local, values_local = project_pair(flat_rows)
    running = absorb(initial, keys_local, values_local)
    held_rows = flat_rows
    for bit_index in range(row_bits):
        partner = swapped(held_rows, "tile", frame_bits + bit_index)
        key_part, value_part = project_pair(partner)
        running = absorb(running, key_part, value_part)
        if bit_index + 1 < row_bits:
            held_rows = jnp.concatenate([held_rows, partner], axis=0)
    highest, weight_sum, numerator = running
    attended = (numerator / weight_sum[:, None]).astype(jnp.bfloat16)
    output_term = jnp.dot(attended, w_output, preferred_element_type=jnp.float32).reshape(
        video_latent.shape
    )
    return (residual.astype(jnp.float32) + output_term).astype(jnp.bfloat16)


def solution(mesh):
    placed = (
        P(("groups", "tile"), None, None),
        P(("groups", "tile"), None, None),
        P(),
        P(),
        P(),
        P(),
        P(),
        P(),
        P(),
    )
    return jax.shard_map(
        body,
        mesh=mesh,
        in_specs=placed,
        out_specs=P(("groups", "tile"), None, None),
        check_vma=False,
    )
```

profile of v0, /device:TPU:0, one launch (start us, length us, event | category | flops | bytes accessed | tf_op | source)
XLA Modules:
  0.0 184.5 jit_solution(8031781905897827496)
XLA Ops:
  4.2 14.1 %collective-permute-done = bf16[2,3,160,384]{3,2,1,0:T(8,128)(2,1)S(1)} collective-permute-done((bf16[2,3,160,384]{3,2,1,0:T(8,128)(2,1)S(1)}, bf16[2,3,160,384]{3,2,1,0:T(8,128)(2,1)S(1)}, u32[]{:S(2)}, u32[]{:S(2)}) %collective-permute-start) | collective-permute-done | bytes 737312 | tf_op jit(solution)/shard_map/ppermute | solution.py:10
  19.6 12.2 %collective-permute-done.1 = bf16[2,3,160,384]{3,2,1,0:T(8,128)(2,1)S(1)} collective-permute-done((bf16[2,3,160,384]{3,2,1,0:T(8,128)(2,1)S(1)}, bf16[2,3,160,384]{3,2,1,0:T(8,128)(2,1)S(1)}, u32[]{:S(2)}, u32[]{:S(2)}) %collective-permute-start.1) | collective-permute-done | bytes 737312 | tf_op jit(solution)/shard_map/ppermute | solution.py:10
  32.0 1.3 collective-permute-start.2
  34.7 1.3 fusion.76
  36.0 1.3 fusion.94
  37.4 9.1 %collective-permute-done.2 = bf16[3,1,160,384]{3,2,1,0:T(8,128)(2,1)S(1)} collective-permute-done((bf16[3,1,160,384]{3,2,1,0:T(8,128)(2,1)S(1)}, bf16[3,1,160,384]{3,2,1,0:T(8,128)(2,1)S(1)}, u32[]{:S(2)}, u32[]{:S(2)}) %collective-permute-start.2) | collective-permute-done | bytes 368672 | tf_op jit(solution)/shard_map/ppermute | solution.py:16
  46.5 1.7 select_maximum_fusion
  59.6 1.4 fusion.42
  62.4 2.5 %collective-permute-start.4 = (bf16[480,384]{1,0:T(8,128)(2,1)S(1)}, bf16[480,384]{1,0:T(8,128)(2,1)S(1)}, u32[]{:S(2)}, u32[]{:S(2)}) collective-permute-start(bf16[480,384]{1,0:T(8,128)(2,1)S(1)} %bitcast.167), channel_id=1, source_target_pairs={{0,2},{1,3},{2,0},{3,1},{4,6},{5,7},{6,4},{7,5},{8,10},{9,11},{10,... | collective-permute-start | bytes 1105928 | tf_op jit(solution)/shard_map/ppermute | solution.py:22
  65.0 5.6 %collective-permute-done.4 = bf16[480,384]{1,0:T(8,128)(2,1)S(1)} collective-permute-done((bf16[480,384]{1,0:T(8,128)(2,1)S(1)}, bf16[480,384]{1,0:T(8,128)(2,1)S(1)}, u32[]{:S(2)}, u32[]{:S(2)}) %collective-permute-start.4) | collective-permute-done | bytes 368672 | tf_op jit(solution)/shard_map/ppermute | solution.py:22
  70.6 5.0 %collective-permute-start.5 = (bf16[960,384]{1,0:T(8,128)(2,1)S(1)}, bf16[960,384]{1,0:T(8,128)(2,1)S(1)}, u32[]{:S(2)}, u32[]{:S(2)}) collective-permute-start(bf16[960,384]{1,0:T(8,128)(2,1)S(1)} %pad_maximum_fusion.2), channel_id=1, source_target_pairs={{0,4},{1,5},{2,6},{3,7},{4,0},{5,1},{6,2},{7,3},{8,12},{9,13},{10,... | collective-permute-start | bytes 2211848 | tf_op jit(solution)/shard_map/ppermute | solution.py:22
  75.7 15.8 %collective-permute-done.5 = bf16[960,384]{1,0:T(8,128)(2,1)S(1)} collective-permute-done((bf16[960,384]{1,0:T(8,128)(2,1)S(1)}, bf16[960,384]{1,0:T(8,128)(2,1)S(1)}, u32[]{:S(2)}, u32[]{:S(2)}) %collective-permute-start.5) | collective-permute-done | bytes 737312 | tf_op jit(solution)/shard_map/ppermute | solution.py:22
  91.5 1.4 pad_maximum_fusion
  92.9 2.8 %collective-permute-start.6 = (bf16[1920,384]{1,0:T(8,128)(2,1)}, bf16[1920,384]{1,0:T(8,128)(2,1)}, u32[]{:S(2)}, u32[]{:S(2)}) collective-permute-start(bf16[1920,384]{1,0:T(8,128)(2,1)} %pad_maximum_fusion), channel_id=1, source_target_pairs={{0,8},{1,9},{2,10},{3,11},{4,12},{5,13},{6,14},{7,15},{8,0},{9,1},... | collective-permute-start | bytes 4423688 | tf_op jit(solution)/shard_map/ppermute | solution.py:22
  97.5 1.9 %fusion.155 = (f32[480]{0:T(512)S(1)}, f32[480,480]{0,1:T(8,128)S(1)}) fusion(bf16[480,384]{1,0:T(8,128)(2,1)} %copy-done.2, bf16[480,384]{1,0:T(8,128)(2,1)S(1)} %collective-permute-done.4, bf16[384,384]{1,0:T(8,128)(2,1)S(1)} %copy-done), kind=kOutput, calls=%fused_computation.206 | convolution fusion | flops 319149600 | bytes 1955712 | tf_op jit(solution)/shard_map/qc,kc->qk/dot_general | solution.py:83
  99.4 3.7 %multiply_reduce_fusion.1 = (f32[480]{0:T(512)S(1)}, f32[480,960]{1,0:T(8,128)}) fusion(bf16[480,384]{1,0:T(8,128)(2,1)} %copy-done.2, bf16[960,384]{1,0:T(8,128)(2,1)} %copy-done.3, bf16[384,384]{1,0:T(8,128)(2,1)S(1)} %copy-done), kind=kOutput, calls=%fused_computation.17 | convolution fusion | flops 638299648 | bytes 3245952 | tf_op jit(solution)/shard_map/qc,kc->qk/dot_general | solution.py:83
  103.2 55.3 %collective-permute-done.6 = bf16[1920,384]{1,0:T(8,128)(2,1)} collective-permute-done((bf16[1920,384]{1,0:T(8,128)(2,1)}, bf16[1920,384]{1,0:T(8,128)(2,1)}, u32[]{:S(2)}, u32[]{:S(2)}) %collective-permute-start.6) | collective-permute-done | bytes 1474592 | tf_op jit(solution)/shard_map/ppermute | solution.py:22
  158.5 5.3 %multiply_reduce_fusion = (f32[480]{0:T(512)S(1)}, f32[480,1920]{1,0:T(8,128)}) fusion(bf16[480,384]{1,0:T(8,128)(2,1)} %copy-done.2, bf16[1920,384]{1,0:T(8,128)(2,1)} %collective-permute-done.6, bf16[384,384]{1,0:T(8,128)(2,1)S(1)} %copy-done), kind=kOutput, calls=%fused_computation.4 | convolution fusion | flops 1276599808 | bytes 5826432 | tf_op jit(solution)/shard_map/qc,kc->qk/dot_general | solution.py:83
  163.8 2.0 %fusion.12 = f32[480]{0:T(512)S(1)} fusion(f32[480,960]{1,0:T(8,128)} %get-tuple-element.45, f32[480]{0:T(512)S(1)} %get-tuple-element.10), kind=kLoop, calls=%fused_computation.21 | loop fusion | flops 1381920 | bytes 1847040 | tf_op jit(solution)/shard_map/reduce_sum | solution.py:89
  165.9 2.8 %fusion.1 = f32[480]{0:T(512)S(1)} fusion(f32[480,1920]{1,0:T(8,128)} %get-tuple-element.43, f32[480]{0:T(512)S(1)} %get-tuple-element.9), kind=kLoop, calls=%fused_computation.5 | loop fusion | flops 2764320 | bytes 3690240 | tf_op jit(solution)/shard_map/reduce_sum | solution.py:89
  169.0 2.7 %fusion.30 = f32[480,384]{1,0:T(8,128)} fusion(bf16[480,384]{1,0:T(8,128)(2,1)S(1)} %bitcast.172, bf16[384,384]{1,0:T(8,128)(2,1)} %param.16, f32[480,480]{0,1:T(8,128)S(1)} %get-tuple-element.49, f32[480]{0:T(512)S(1)} %get-tuple-element.41, f32[480]{0:T(512)S(1)} %get-tuple-element.8, f32[480]{0:T(512)S(1)} %get-tuple-element.40), kind=kOutput, calls=%fused_computation.48 | convolution fusion | flops 319518720 | bytes 2328192 | tf_op jit(solution)/shard_map/dot_general | solution.py:90
  171.6 3.9 %fusion.35 = f32[480,384]{1,0:T(8,128)} fusion(bf16[960,384]{1,0:T(8,128)(2,1)} %copy-done.3, bf16[384,384]{1,0:T(8,128)(2,1)} %param.16, f32[480,960]{1,0:T(8,128)} %get-tuple-element.45, f32[480]{0:T(512)S(1)} %get-tuple-element.10), kind=kOutput, calls=%fused_computation.53 | convolution fusion | flops 638760960 | bytes 3614592 | tf_op jit(solution)/shard_map/dot_general | solution.py:90
  175.5 5.4 %fusion.8 = f32[480,384]{1,0:T(8,128)} fusion(f32[480,1920]{1,0:T(8,128)} %get-tuple-element.43, f32[480]{0:T(512)S(1)} %get-tuple-element.9, bf16[1920,384]{1,0:T(8,128)(2,1)} %collective-permute-done.6, bf16[384,384]{1,0:T(8,128)(2,1)S(1)} %copy-done.7), kind=kOutput, calls=%fused_computation.18 | convolution fusion | flops 1277521920 | bytes 6195072 | tf_op jit(solution)/shard_map/dot_general | solution.py:90
  180.9 2.4 %fusion.44 = bf16[480,384]{1,0:T(8,128)(2,1)S(1)} fusion(f32[480,384]{1,0:T(8,128)} %fusion.8, f32[480,384]{1,0:T(8,128)} %fusion.35, f32[480,384]{1,0:T(8,128)} %fusion.30, bf16[480,384]{1,0:T(8,128)(2,1)S(1)} %collective-permute-done.4, bf16[384,384]{1,0:T(8,128)(2,1)S(1)} %copy-done.7, f32[480,480]{0,1:T(8,128)S(1)} %get-tuple-element.47, ...), kind=kOutput, calls=%fused_computation.67 | convolution fusion | flops 320440320 | bytes 4173312 | tf_op jit(solution)/shard_map/dot_general | solution.py:90
  (71 shorter events, 22.9 us)
Async XLA Ops:
  0.0 96.8 %copy-start = (bf16[384,384]{1,0:T(8,128)(2,1)S(1)}, bf16[384,384]{1,0:T(8,128)(2,1)}, u32[]{:S(2)}) copy-start(bf16[384,384]{1,0:T(8,128)(2,1)} %param.15) | copy-start | bytes 884740
  3.6 14.7 %collective-permute-start = (bf16[2,3,160,384]{3,2,1,0:T(8,128)(2,1)S(1)}, bf16[2,3,160,384]{3,2,1,0:T(8,128)(2,1)S(1)}, u32[]{:S(2)}, u32[]{:S(2)}) collective-permute-start(bf16[2,3,160,384]{3,2,1,0:T(8,128)(2,1)S(1)} %pad_maximum_fusion.1), channel_id=1, source_target_pairs={{0,1},{1,2},{2,3},{3,4},{4,5},{5,6},{6,7},{7,8},{8,9},{9,10},{10,1... | collective-permute-start | bytes 2211848 | tf_op jit(solution)/shard_map/ppermute | solution.py:10
  18.3 13.6 %collective-permute-start.1 = (bf16[2,3,160,384]{3,2,1,0:T(8,128)(2,1)S(1)}, bf16[2,3,160,384]{3,2,1,0:T(8,128)(2,1)S(1)}, u32[]{:S(2)}, u32[]{:S(2)}) collective-permute-start(bf16[2,3,160,384]{3,2,1,0:T(8,128)(2,1)S(1)} %collective-permute-done), channel_id=1, source_target_pairs={{0,1},{1,2},{2,3},{3,4},{4,5},{5,6},{6,7},{7,8},{8,9},{9,10},{10,1... | collective-permute-start | bytes 2211848 | tf_op jit(solution)/shard_map/ppermute | solution.py:10
  32.0 14.4 %collective-permute-start.2 = (bf16[3,1,160,384]{3,2,1,0:T(8,128)(2,1)S(1)}, bf16[3,1,160,384]{3,2,1,0:T(8,128)(2,1)S(1)}, u32[]{:S(2)}, u32[]{:S(2)}) collective-permute-start(bf16[3,1,160,384]{3,2,1,0:T(8,128)(2,1)S(1)} %get-tuple-element.38), channel_id=1, source_target_pairs={{0,2},{1,3},{2,4},{3,5},{4,6},{5,7},{6,8},{7,9},{8,10},{9,11},{10,... | collective-permute-start | bytes 1105928 | tf_op jit(solution)/shard_map/ppermute | solution.py:16
  33.4 13.1 %collective-permute-start.3 = (bf16[3,1,160,384]{3,2,1,0:T(8,128)(2,1)S(1)}, bf16[3,1,160,384]{3,2,1,0:T(8,128)(2,1)S(1)}, u32[]{:S(2)}, u32[]{:S(2)}) collective-permute-start(bf16[3,1,160,384]{3,2,1,0:T(8,128)(2,1)S(1)} %get-tuple-element.39), channel_id=1, source_target_pairs={{2,0},{3,1},{4,2},{5,3},{6,4},{7,5},{8,6},{9,7},{10,8},{11,9},{12,... | collective-permute-start | bytes 1105928 | tf_op jit(solution)/shard_map/ppermute | solution.py:16
  46.5 2.8 %slice-start = ((s8[7962624]{0:T(1024)(128)(4,1)}), s8[4194304]{0:T(1024)(128)(4,1)S(1)}, s32[]{:S(2)}) async-start(s8[7962624]{0:T(1024)(128)(4,1)} %bitcast.173), calls=%async_computation | async-start | bytes 8388608
  48.2 2.2 %slice-start.1 = ((s8[7962624]{0:T(1024)(128)(4,1)}), s8[3768320]{0:T(1024)(128)(4,1)S(1)}, s32[]{:S(2)}) async-start(s8[7962624]{0:T(1024)(128)(4,1)} %bitcast.173), calls=%async_computation.1 | async-start | bytes 7536640
  61.0 1.0 copy-start.1
  61.0 1.2 copy-start.6
  61.5 34.2 %copy-start.4 = (bf16[384,384]{1,0:T(8,128)(2,1)S(1)}, bf16[384,384]{1,0:T(8,128)(2,1)}, u32[]{:S(2)}) copy-start(bf16[384,384]{1,0:T(8,128)(2,1)} %param.14) | copy-start | bytes 884740
  62.4 8.2 %collective-permute-start.4 = (bf16[480,384]{1,0:T(8,128)(2,1)S(1)}, bf16[480,384]{1,0:T(8,128)(2,1)S(1)}, u32[]{:S(2)}, u32[]{:S(2)}) collective-permute-start(bf16[480,384]{1,0:T(8,128)(2,1)S(1)} %bitcast.167), channel_id=1, source_target_pairs={{0,2},{1,3},{2,0},{3,1},{4,6},{5,7},{6,4},{7,5},{8,10},{9,11},{10,... | collective-permute-start | bytes 1105928 | tf_op jit(solution)/shard_map/ppermute | solution.py:22
  70.6 20.8 %collective-permute-start.5 = (bf16[960,384]{1,0:T(8,128)(2,1)S(1)}, bf16[960,384]{1,0:T(8,128)(2,1)S(1)}, u32[]{:S(2)}, u32[]{:S(2)}) collective-permute-start(bf16[960,384]{1,0:T(8,128)(2,1)S(1)} %pad_maximum_fusion.2), channel_id=1, source_target_pairs={{0,4},{1,5},{2,6},{3,7},{4,0},{5,1},{6,2},{7,3},{8,12},{9,13},{10,... | collective-permute-start | bytes 2211848 | tf_op jit(solution)/shard_map/ppermute | solution.py:22
  91.5 4.2 %copy-start.3 = (bf16[960,384]{1,0:T(8,128)(2,1)}, bf16[960,384]{1,0:T(8,128)(2,1)S(1)}, u32[]{:S(2)}) copy-start(bf16[960,384]{1,0:T(8,128)(2,1)S(1)} %collective-permute-done.5) | copy-start | bytes 2211844
  92.9 65.6 %collective-permute-start.6 = (bf16[1920,384]{1,0:T(8,128)(2,1)}, bf16[1920,384]{1,0:T(8,128)(2,1)}, u32[]{:S(2)}, u32[]{:S(2)}) collective-permute-start(bf16[1920,384]{1,0:T(8,128)(2,1)} %pad_maximum_fusion), channel_id=1, source_target_pairs={{0,8},{1,9},{2,10},{3,11},{4,12},{5,13},{6,14},{7,15},{8,0},{9,1},... | collective-permute-start | bytes 4423688 | tf_op jit(solution)/shard_map/ppermute | solution.py:22
  96.0 0.7 copy-start.2
  171.6 3.9 %copy-start.7 = (bf16[384,384]{1,0:T(8,128)(2,1)S(1)}, bf16[384,384]{1,0:T(8,128)(2,1)}, u32[]{:S(2)}) copy-start(bf16[384,384]{1,0:T(8,128)(2,1)} %param.16) | copy-start | bytes 884740
  180.9 2.4 %copy-start.5 = (bf16[384,384]{1,0:T(8,128)(2,1)S(1)}, bf16[384,384]{1,0:T(8,128)(2,1)}, u32[]{:S(2)}) copy-start(bf16[384,384]{1,0:T(8,128)(2,1)} %param.17) | copy-start | bytes 884740
where the time goes:
time: 185 us
  waiting for transfers between devices  112 us (61%)
  matrix products  40 us (22%)
  other arithmetic  15 us (8%)
  starting transfers between devices  13.5 us (7%)
  local copies, waits for them, and re-layouts  3.47 us (2%)
    ppermute x3, waiting for transfers between devices, swapped(): return lax.ppermute(value, axis, pairs)  76.7 us
    ppermute x2, waiting for transfers between devices, from_behind(): return lax.ppermute(value, axis, pairs)  26.4 us
    dot_general x4, matrix products, absorb(): jnp.dot(weights.astype(jnp.bfloat16), value_part, preferred_element_type=...  14.3 us
    dot_general x27, matrix products, body(): jnp.dot(window.reshape(-1, channels), conv_kernel[time_tap, row_tap, col_...  13.2 us
    dot_general x4, matrix products, absorb(): jnp.einsum('qc,kc->qk', queries, key_part, preferred_element_type=jnp.flo...  11.7 us
    ppermute x3, starting transfers between devices, swapped(): return lax.ppermute(value, axis, pairs)  10.3 us
    ppermute x2, waiting for transfers between devices, passed_along(): return lax.ppermute(block, axis, route)  9.11 us
    reduce_sum x3, other arithmetic, absorb(): weight_sum = weight_sum * rescale + jnp.sum(weights, axis=-1)  5.12 us
  transfers between devices with their start and end apart: 7, of which 6 were waited for; matrix products, arithmetic and copies ran while one was open for 6% of the time, Pallas kernels for 0%

commit v1 on v0

v1 whole, which is shorter than its diff:
```python
import functools

import jax
import jax.numpy as jnp
from jax import lax
from jax.experimental import pallas as pl
from jax.experimental.pallas import tpu as pltpu
from jax.sharding import PartitionSpec as P

LOG2E = 1.4426950408889634
F32 = jnp.float32
BF16 = jnp.bfloat16


def params(mib, **kw):
    return pltpu.CompilerParams(vmem_limit_bytes=mib * 2**20, **kw)


def rms(values, gain):
    floats = values.astype(F32)
    return floats * lax.rsqrt(jnp.mean(floats * floats, axis=-1, keepdims=True) + 1e-06) * gain


def silu(values):
    return values / (1.0 + jnp.exp(-values))


def tap_product(rows, cols, lhs_ref, w_ref):
    span = rows * cols
    lhs = jnp.concatenate([lhs_ref[pl.ds(i * cols, span), :] for i in range(3)], axis=1)
    rhs = jnp.concatenate([w_ref[i] for i in range(3)], axis=0)
    return jnp.dot(lhs, rhs, preferred_element_type=F32)


def add_tap(rows, cols, total, product):
    span = rows * cols
    column = lax.broadcasted_iota(jnp.int32, product.shape, 0) % cols
    tap = pl.program_id(0)

    @pl.when(tap == 0)
    def _():
        total[...] += jnp.where(column == 0, 0.0, pltpu.roll(product, 1, 0))

    @pl.when(tap == 1)
    def _():
        total[...] += product

    @pl.when(tap == 2)
    def _():
        total[...] += jnp.where(column == cols - 1, 0.0, pltpu.roll(product, span - 1, 0))


def own_kernel(rows, cols, x_ref, above_ref, below_ref, gain_ref, w_ref, act_ref, total_ref):
    @pl.when(pl.program_id(0) == 0)
    def _():
        gain = gain_ref[...]
        act_ref[pl.ds(0, cols), :] = silu(rms(above_ref[...], gain)).astype(BF16)
        act_ref[pl.ds(cols, rows * cols), :] = silu(rms(x_ref[...], gain)).astype(BF16)
        act_ref[pl.ds((rows + 1) * cols, cols), :] = silu(rms(below_ref[...], gain)).astype(BF16)
        total_ref[...] = jnp.zeros_like(total_ref)

    add_tap(rows, cols, total_ref, tap_product(rows, cols, act_ref, w_ref))


def middle_kernel(rows, cols, in_ref, w_ref, before_ref, total_ref):
    @pl.when(pl.program_id(0) == 0)
    def _():
        total_ref[...] = before_ref[...]

    add_tap(rows, cols, total_ref, tap_product(rows, cols, in_ref, w_ref))


def last_kernel(rows, cols, in_ref, w_ref, before_ref, x_ref, gain_ref, res_ref, normed_ref, total):
    @pl.when(pl.program_id(0) == 0)
    def _():
        total[...] = before_ref[...] + x_ref[...].astype(F32)

    add_tap(rows, cols, total, tap_product(rows, cols, in_ref, w_ref))

    @pl.when(pl.program_id(0) == 2)
    def _():
        residual = total[...].astype(BF16)
        res_ref[...] = residual
        normed_ref[...] = rms(residual, gain_ref[...]).astype(BF16)


def whole(shape):
    return pl.BlockSpec(shape, lambda *_: (0,) * len(shape))


def weight_spec(time_tap, channels):
    return pl.BlockSpec(
        (None, 3, None, channels, channels), lambda tap: (time_tap, 0, tap, 0, 0)
    )


def score_part(query, key):
    return lax.dot_general(
        query, key, (((1,), (1,)), ((), ())), preferred_element_type=F32
    )


def first_kernel(scale, normed_ref, wq_ref, wk_ref, query_ref, high_ref, sum_ref, acc_ref):
    keys = normed_ref[...]
    query = jnp.dot(keys, wq_ref[...], preferred_element_type=F32).astype(BF16)
    query = (score_part(query, wk_ref[...]) * scale).astype(BF16)
    query_ref[...] = query
    scores = score_part(query, keys)
    high = jnp.max(scores, axis=-1, keepdims=True)
    weights = jnp.exp2(scores - high)
    high_ref[...] = jnp.broadcast_to(high, high_ref.shape)
    sum_ref[...] = jnp.broadcast_to(jnp.sum(weights, axis=-1, keepdims=True), sum_ref.shape)
    acc_ref[...] = jnp.dot(weights.astype(BF16), keys, preferred_element_type=F32)


def absorb(query, blocks, high_before, sum_before, acc_before):
    scores = [score_part(query, keys) for keys in blocks]
    high = high_before
    for part in scores:
        high = jnp.maximum(high, jnp.max(part, axis=-1, keepdims=True))
    rescale = jnp.exp2(high_before - high)
    total = sum_before * rescale
    acc = acc_before * rescale
    for part, keys in zip(scores, blocks):
        weights = jnp.exp2(part - high)
        total = total + jnp.sum(weights, axis=-1, keepdims=True)
        acc = acc + jnp.dot(weights.astype(BF16), keys, preferred_element_type=F32)
    return high, total, acc


def more_kernel(count, query_ref, *refs):
    blocks, (high_ref, sum_ref, acc_ref), (high_out, sum_out, acc_out) = (
        refs[:count], refs[count : count + 3], refs[count + 3 :]
    )
    high, total, acc = absorb(
        query_ref[...], [ref[...] for ref in blocks], high_ref[:, :1], sum_ref[:, :1], acc_ref[...]
    )
    high_out[...] = jnp.broadcast_to(high, high_out.shape)
    sum_out[...] = jnp.broadcast_to(total, sum_out.shape)
    acc_out[...] = acc


def final_kernel(count, query_ref, *refs):
    blocks, (high_ref, sum_ref, acc_ref, res_ref, wv_ref, wo_ref, out_ref) = (
        refs[:count], refs[count:]
    )
    _, total, acc = absorb(
        query_ref[...], [ref[...] for ref in blocks], high_ref[:, :1], sum_ref[:, :1], acc_ref[...]
    )
    mixed = (acc / total).astype(BF16)
    attended = jnp.dot(mixed, wv_ref[...], preferred_element_type=F32).astype(BF16)
    term = jnp.dot(attended, wo_ref[...], preferred_element_type=F32)
    out_ref[...] = (res_ref[...].astype(F32) + term).astype(BF16)


def ring_order(row_tiles):
    half = row_tiles // 2
    return [2 * k for k in range(half)] + [2 * (half - 1 - k) + 1 for k in range(half)]


def body(
    video_latent, conv_cache, norm_gain, conv_kernel, attend_gain, w_query, w_key, w_value, w_output
):
    rows, cols, channels = video_latent.shape
    span = rows * cols
    tiles = lax.axis_size("tile")
    row_tiles = min(16, tiles // 2)
    frames = tiles // row_tiles
    position = lax.axis_index("tile")
    frame = position % frames
    tile = position // frames

    def send(value, moves):
        pairs = [(a * frames + s, b * frames + t) for (a, s), (b, t) in moves]
        return lax.ppermute(value, "tile", pairs)

    flat = video_latent.reshape(span, channels)
    cache = conv_cache.reshape(span, channels)
    all_tiles = range(row_tiles)
    cached = [(frames - 2 + t, t) for t in range(2)]

    cache_block = send(
        cache, [(((r - 1) % row_tiles, s), (r, t)) for r in all_tiles for s, t in cached]
    )
    cache_above = send(
        cache[span - cols :],
        [(((r - 2) % row_tiles, s), (r, t)) for r in all_tiles[1:] for s, t in cached],
    )
    above = send(
        flat[span - cols :],
        [((r - 1, t), (r, t)) for r in all_tiles[1:] for t in range(frames)],
    )
    below = send(
        flat[:cols], [((r + 1, t), (r, t)) for r in all_tiles[:-1] for t in range(frames)]
    )
    if frames == 2:
        cache_below = jnp.where(tile < row_tiles - 1, cache[:cols], 0).astype(BF16)
    else:
        cache_below = send(
            cache[:cols], [((r, s), (r, t)) for r in all_tiles[:-1] for s, t in cached]
        )

    gain = norm_gain.reshape(1, channels)
    wide = jax.ShapeDtypeStruct((span, channels), F32)
    narrow = jax.ShapeDtypeStruct((span, channels), BF16)
    padded = jax.ShapeDtypeStruct((span + 2 * cols, channels), BF16)
    full, rim, tall, row = (span, channels), (cols, channels), padded.shape, (1, channels)
    conv_flops = 2 * span * 9 * channels * channels
    conv_cost = pl.CostEstimate(
        flops=conv_flops, bytes_accessed=18 * channels * channels, transcendentals=0
    )

    act, total = pl.pallas_call(
        functools.partial(own_kernel, rows, cols),
        grid=(3,),
        out_shape=(padded, wide),
        in_specs=[whole(full), whole(rim), whole(rim), whole(row), weight_spec(2, channels)],
        out_specs=(whole(tall), whole(full)),
        compiler_params=params(24),
        cost_estimate=conv_cost,
        name="conv_own",
    )(flat, above, below, gain, conv_kernel)

    cache_all = jnp.concatenate([cache_above, cache_block, cache_below], axis=0)
    if frames == 2:
        swap = jnp.where(frame == 0, act, cache_all)
        two_back = cache_all
        one_back = send(swap, [((r, t), (r, 1 - t)) for r in all_tiles for t in range(2)])
    else:
        later = send(
            act, [((r, t), (r, t + 1)) for r in all_tiles for t in range(frames - 1)]
        )
        first = send(cache_all, [((r, 1), (r, 0)) for r in all_tiles])
        one_back = jnp.where(frame == 0, first, later)
        earlier = send(
            act, [((r, t), (r, t + 2)) for r in all_tiles for t in range(frames - 2)]
        )
        two_back = jnp.where(frame < 2, cache_all, earlier)

    total = pl.pallas_call(
        functools.partial(middle_kernel, rows, cols),
        grid=(3,),
        out_shape=wide,
        in_specs=[whole(tall), weight_spec(0, channels), whole(full)],
        out_specs=whole(full),
        compiler_params=params(24),
        cost_estimate=conv_cost,
        name="conv_two_back",
    )(two_back, conv_kernel, total)

    residual, normed = pl.pallas_call(
        functools.partial(last_kernel, rows, cols),
        grid=(3,),
        out_shape=(narrow, narrow),
        in_specs=[
            whole(tall), weight_spec(1, channels), whole(full), whole(full), whole(row),
        ],
        out_specs=(whole(full), whole(full)),
        scratch_shapes=[pltpu.VMEM(full, F32)],
        compiler_params=params(24),
        cost_estimate=conv_cost,
        name="conv_one_back",
    )(one_back, conv_kernel, total, flat, attend_gain.reshape(1, channels))

    order = ring_order(row_tiles)
    forward = [
        ((order[k], t), (order[(k + 1) % row_tiles], t)) for k in all_tiles for t in range(frames)
    ]
    backward = [(b, a) for a, b in forward]
    arrived, right, left = [], normed, normed
    for _ in range(row_tiles // 2 - 1):
        right, left = send(right, forward), send(left, backward)
        arrived.append((right, left))
    cut = span // 2
    arrived.append((send(right[:cut], forward), send(left[cut:], backward)))

    stat = jax.ShapeDtypeStruct((span, 128), F32)
    scale = LOG2E * float(channels) ** (-0.5)
    attend_cost = lambda keys: pl.CostEstimate(
        flops=4 * span * keys * channels, bytes_accessed=2 * keys * channels,
        transcendentals=span * keys,
    )
    query, high, weight_sum, acc = pl.pallas_call(
        functools.partial(first_kernel, scale),
        out_shape=(narrow, stat, stat, wide),
        compiler_params=params(24),
        cost_estimate=attend_cost(span),
        name="attend_own",
    )(normed, w_query, w_key)
    for blocks in arrived[:-1]:
        high, weight_sum, acc = pl.pallas_call(
            functools.partial(more_kernel, len(blocks)),
            out_shape=(stat, stat, wide),
            compiler_params=params(24),
            cost_estimate=attend_cost(2 * span),
            name="attend_more",
        )(query, *blocks, high, weight_sum, acc)
    blocks = arrived[-1]
    result = pl.pallas_call(
        functools.partial(final_kernel, len(blocks)),
        out_shape=narrow,
        compiler_params=params(24),
        cost_estimate=attend_cost(span),
        name="attend_last",
    )(query, *blocks, high, weight_sum, acc, residual, w_value, w_output)
    return result.reshape(video_latent.shape)


def solution(mesh):
    spread = P(("groups", "tile"), None, None)
    return jax.shard_map(
        body,
        mesh=mesh,
        in_specs=(spread, spread) + (P(),) * 7,
        out_specs=spread,
        check_vma=False,
    )
```

time: 185 us -> 72.7 us (0.39)
  waiting for transfers between devices: 112 us -> 24.3 us
  matrix products: 40 us -> 0 us
  Pallas kernels: 0 us -> 19.3 us
  other arithmetic: 15 us -> 1.22 us
  starting transfers between devices: 13.5 us -> 22.1 us
  local copies, waits for them, and re-layouts: 3.47 us -> 5.37 us
    ppermute x7 -> x13, waiting for transfers between devices: 112 us -> 24.3 us  [send(): return lax.ppermute(value, 'tile', pairs)]
    dot_general x37 -> x0, matrix products: 40 us -> none  [the longest x4 14.3 us: absorb(): jnp.dot(weights.astype(jnp.bfloat16), value_part, preferred_element_type=...]
    pallas_call x0 -> x8, Pallas kernels: none -> 19.3 us  [the longest x3 5.25 us: body(): pl.pallas_call(functools.partial(more_kernel, len(blocks)), out_shape=(st...]
    ppermute x7 -> x13, starting transfers between devices: 13.5 us -> 22.1 us  [send(): return lax.ppermute(value, 'tile', pairs)]
    reduce_sum x5 -> x0, other arithmetic: 6.54 us -> none  [the longest x3 5.12 us: absorb(): weight_sum = weight_sum * rescale + jnp.sum(weights, axis=-1)]
    concatenate x3 -> x1, other arithmetic: 3.21 us -> 0.23 us  [body(): cache_all = jnp.concatenate([cache_above, cache_block, cache_below], axis=0)]
    another operation x2 -> x0, other arithmetic: 2.37 us -> none  [body(): frame_pair = jnp.stack([activated, conv_cache])]
    convert_element_type x3 -> x0, other arithmetic: 2.25 us -> none  [the longest x1 1.28 us: body(): jax.nn.silu(rms_scale(video_latent, norm_gain)).astype(jnp.bfloat16)]
  transfers between devices with their start and end apart: 7 -> 13, of which waited for: 6 -> 5; matrix products, arithmetic and copies ran while one was open for 6% -> 4% of each run, Pallas kernels for 0% -> 19%
where the time goes in v1:
time: 72.7 us; the launch traced here: 72.4 us
  waiting for transfers between devices  24.3 us (33%)
  starting transfers between devices  22.1 us (30%)
  Pallas kernels  19.3 us (27%)
  local copies, waits for them, and re-layouts  5.37 us (7%)
  other arithmetic  1.22 us (2%)
    ppermute x13, waiting for transfers between devices, send(): return lax.ppermute(value, 'tile', pairs)  24.3 us
    ppermute x13, starting transfers between devices, send(): return lax.ppermute(value, 'tile', pairs)  22.1 us
    pallas_call x3, Pallas kernels, body(): pl.pallas_call(functools.partial(more_kernel, len(blocks)), out_shape=(st...  5.25 us
    pallas_call x1, Pallas kernels, body(): pl.pallas_call(functools.partial(own_kernel, rows, cols), grid=(3,), out_...  3.73 us
    unnamed x16, local copies, waits for them, and re-layouts  3.65 us
    pallas_call x1, Pallas kernels, body(): pl.pallas_call(functools.partial(last_kernel, rows, cols), grid=(3,), out...  3.39 us
    pallas_call x1, Pallas kernels, body(): pl.pallas_call(functools.partial(middle_kernel, rows, cols), grid=(3,), o...  3.19 us
    pallas_call x1, Pallas kernels, body(): pl.pallas_call(functools.partial(final_kernel, len(blocks)), out_shape=na...  2.41 us
  transfers between devices with their start and end apart: 13, of which 5 were waited for; matrix products, arithmetic and copies ran while one was open for 4% of the time, Pallas kernels for 19%

profile of v1, /device:TPU:0, one launch (start us, length us, event | category | flops | bytes accessed | tf_op | source)
XLA Modules:
  0.0 72.4 jit_solution(15384082625886089010)
XLA Ops:
  0.0 3.0 %collective-permute-start.3 = (bf16[480,384]{1,0:T(8,128)(2,1)}, bf16[480,384]{1,0:T(8,128)(2,1)S(1)}, u32[]{:S(2)}, u32[]{:S(2)}) collective-permute-start(bf16[480,384]{1,0:T(8,128)(2,1)} %bitcast.13), channel_id=1, source_target_pairs={{14,0},{15,1},{0,2},{1,3},{2,4},{3,5},{4,6},{5,7},{6,8},{7,9},{8,1... | collective-permute-start | bytes 1105928 | tf_op jit(solution)/shard_map/ppermute | solution.py:175
  3.0 1.0 %slice_bitcast_fusion.1 = (bf16[160,384]{1,0:T(8,128)(2,1)S(1)}, bf16[160,384]{1,0:T(8,128)(2,1)S(1)}) fusion(bf16[3,160,384]{2,1,0:T(8,128)(2,1)} %param.9), kind=kLoop, calls=%fused_computation.4 | loop fusion | bytes 491520 | tf_op jit(solution)/shard_map/slice | solution.py:194
  4.0 3.4 %collective-permute-start = (bf16[160,384]{1,0:T(8,128)(2,1)S(1)}, bf16[160,384]{1,0:T(8,128)(2,1)S(1)}, u32[]{:S(2)}, u32[]{:S(2)}) collective-permute-start(bf16[160,384]{1,0:T(8,128)(2,1)S(1)} %get-tuple-element.44), channel_id=1, source_target_pairs={{0,2},{1,3},{2,4},{3,5},{4,6},{5,7},{6,8},{7,9},{8,10},{9,11},{10,... | collective-permute-start | bytes 368648 | tf_op jit(solution)/shard_map/ppermute | solution.py:175
  7.4 1.3 %collective-permute-start.1 = (bf16[160,384]{1,0:T(8,128)(2,1)S(1)}, bf16[160,384]{1,0:T(8,128)(2,1)S(1)}, u32[]{:S(2)}, u32[]{:S(2)}) collective-permute-start(bf16[160,384]{1,0:T(8,128)(2,1)S(1)} %get-tuple-element.43), channel_id=1, source_target_pairs={{2,0},{3,1},{4,2},{5,3},{6,4},{7,5},{8,6},{9,7},{10,8},{11,9},{12,... | collective-permute-start | bytes 368648 | tf_op jit(solution)/shard_map/ppermute | solution.py:175
  8.7 1.0 %slice_bitcast_fusion = (bf16[160,384]{1,0:T(8,128)(2,1)S(1)}, bf16[160,384]{1,0:T(8,128)(2,1)S(1)}) fusion(bf16[3,160,384]{2,1,0:T(8,128)(2,1)} %param.10, pred[]{:T(512)S(6)} %lt.10), kind=kLoop, calls=%fused_computation.3 | loop fusion | flops 61440 | bytes 491521 | tf_op jit(solution)/shard_map/slice | solution.py:186
  9.7 5.5 %collective-permute-start.2 = (bf16[160,384]{1,0:T(8,128)(2,1)S(1)}, bf16[160,384]{1,0:T(8,128)(2,1)S(1)}, u32[]{:S(2)}, u32[]{:S(2)}) collective-permute-start(bf16[160,384]{1,0:T(8,128)(2,1)S(1)} %get-tuple-element.41), channel_id=1, source_target_pairs={{14,2},{15,3},{0,4},{1,5},{2,6},{3,7},{4,8},{5,9},{6,10},{7,11},{8... | collective-permute-start | bytes 368648 | tf_op jit(solution)/shard_map/ppermute | solution.py:175
  16.3 1.1 %collective-permute-done.1.below_ref = bf16[160,384]{1,0:T(8,128)(2,1)S(1)} collective-permute-done((bf16[160,384]{1,0:T(8,128)(2,1)S(1)}, bf16[160,384]{1,0:T(8,128)(2,1)S(1)}, u32[]{:S(2)}, u32[]{:S(2)}) %collective-permute-start.1) | collective-permute-done | bytes 122912 | tf_op jit(solution)/shard_map/ppermute | solution.py:175
  17.5 3.3 %copy-done = bf16[3,3,3,384,384]{4,3,2,1,0:T(8,128)(2,1)S(1)} copy-done((bf16[3,3,3,384,384]{4,3,2,1,0:T(8,128)(2,1)S(1)}, bf16[3,3,3,384,384]{4,3,2,1,0:T(8,128)(2,1)}, u32[]{:S(2)}) %copy-start) | copy-done | bytes 7962648
  20.7 3.7 %conv_own.1 = (bf16[800,384]{1,0:T(8,128)(2,1)S(1)}, f32[480,384]{1,0:T(8,128)S(1)}) custom-call(bf16[480,384]{1,0:T(8,128)(2,1)S(1)} %bitcast.11, bf16[160,384]{1,0:T(8,128)(2,1)S(1)} %collective-permute-done.above_ref, bf16[160,384]{1,0:T(8,128)(2,1)S(1)} %collective-permute-done.1.below_ref, f32[1,384]{1,0:T(1,128)S(1)} %reshape.23.gain_ref, ...), custom_call_target="tpu_custom_call" | custom-call | flops 1274019840 | bytes 2654208 | tf_op jit(solution)/shard_map/conv_own/pallas_call | solution.py:213
  25.2 3.2 %conv_two_back.1.before_ref = f32[480,384]{1,0:T(8,128)S(1)} custom-call(bf16[800,384]{1,0:T(8,128)(2,1)S(1)} %get-tuple-element.39.in_ref, bf16[3,3,3,384,384]{4,3,2,1,0:T(8,128)(2,1)S(1)} %copy-done.1, f32[480,384]{1,0:T(8,128)S(1)} %get-tuple-element.23.before_ref), custom_call_target="tpu_custom_call" | custom-call | flops 1274019840 | bytes 2654208 | tf_op jit(solution)/shard_map/conv_two_back/pallas_call | solution.py:240
  28.4 3.4 %conv_one_back.1 = (bf16[480,384]{1,0:T(8,128)(2,1)S(1)}, bf16[480,384]{1,0:T(8,128)(2,1)S(1)}) custom-call(bf16[800,384]{1,0:T(8,128)(2,1)S(1)} %collective-permute-done.4.in_ref, bf16[3,3,3,384,384]{4,3,2,1,0:T(8,128)(2,1)S(1)} %copy-done.1, f32[480,384]{1,0:T(8,128)S(1)} %conv_two_back.1.before_ref, bf16[480,384]{1,0:T(8,128)(2,1)S(1)} %bitcast.12, ...), custom_call_target="tpu_custom_call" | custom-call | flops 1274019840 | bytes 2654208 | tf_op jit(solution)/shard_map/conv_one_back/pallas_call | solution.py:251
  31.8 1.4 %collective-permute-start.9 = (bf16[480,384]{1,0:T(8,128)(2,1)S(1)}, bf16[480,384]{1,0:T(8,128)(2,1)S(1)}, u32[]{:S(2)}, u32[]{:S(2)}) collective-permute-start(bf16[480,384]{1,0:T(8,128)(2,1)S(1)} %get-tuple-element.24.normed_ref), channel_id=1, source_target_pairs={{4,0},{5,1},{8,4},{9,5},{12,8},{13,9},{14,12},{15,13},{10,14},{11,... | collective-permute-start | bytes 1105928 | tf_op jit(solution)/shard_map/ppermute | solution.py:175
  33.2 1.0 %collective-permute-start.5 = (bf16[480,384]{1,0:T(8,128)(2,1)S(1)}, bf16[480,384]{1,0:T(8,128)(2,1)S(1)}, u32[]{:S(2)}, u32[]{:S(2)}) collective-permute-start(bf16[480,384]{1,0:T(8,128)(2,1)S(1)} %get-tuple-element.24.normed_ref), channel_id=1, source_target_pairs={{0,4},{1,5},{4,8},{5,9},{8,12},{9,13},{12,14},{13,15},{14,10},{15,... | collective-permute-start | bytes 1105928 | tf_op jit(solution)/shard_map/ppermute | solution.py:175
  34.2 8.8 %collective-permute-done.9.refs_1_ = bf16[480,384]{1,0:T(8,128)(2,1)S(1)} collective-permute-done((bf16[480,384]{1,0:T(8,128)(2,1)S(1)}, bf16[480,384]{1,0:T(8,128)(2,1)S(1)}, u32[]{:S(2)}, u32[]{:S(2)}) %collective-permute-start.9) | collective-permute-done | bytes 368672 | tf_op jit(solution)/shard_map/ppermute | solution.py:175
  43.9 1.2 %collective-permute-start.6 = (bf16[480,384]{1,0:T(8,128)(2,1)S(1)}, bf16[480,384]{1,0:T(8,128)(2,1)S(1)}, u32[]{:S(2)}, u32[]{:S(2)}) collective-permute-start(bf16[480,384]{1,0:T(8,128)(2,1)S(1)} %collective-permute-done.5.refs_0_), channel_id=1, source_target_pairs={{0,4},{1,5},{4,8},{5,9},{8,12},{9,13},{12,14},{13,15},{14,10},{15,... | collective-permute-start | bytes 1105928 | tf_op jit(solution)/shard_map/ppermute | solution.py:175
  45.1 8.0 %collective-permute-done.10.refs_1_ = bf16[480,384]{1,0:T(8,128)(2,1)S(1)} collective-permute-done((bf16[480,384]{1,0:T(8,128)(2,1)S(1)}, bf16[480,384]{1,0:T(8,128)(2,1)S(1)}, u32[]{:S(2)}, u32[]{:S(2)}) %collective-permute-start.10) | collective-permute-done | bytes 368672 | tf_op jit(solution)/shard_map/ppermute | solution.py:175
  53.6 1.5 %collective-permute-start.7 = (bf16[480,384]{1,0:T(8,128)(2,1)S(1)}, bf16[480,384]{1,0:T(8,128)(2,1)S(1)}, u32[]{:S(2)}, u32[]{:S(2)}) collective-permute-start(bf16[480,384]{1,0:T(8,128)(2,1)S(1)} %collective-permute-done.6.refs_0_), channel_id=1, source_target_pairs={{0,4},{1,5},{4,8},{5,9},{8,12},{9,13},{12,14},{13,15},{14,10},{15,... | collective-permute-start | bytes 1105928 | tf_op jit(solution)/shard_map/ppermute | solution.py:175
  55.2 1.3 %attend_own.1 = (bf16[480,384]{1,0:T(8,128)(2,1)S(1)}, f32[480,128]{1,0:T(8,128)S(1)}, f32[480,128]{1,0:T(8,128)S(1)}, f32[480,384]{1,0:T(8,128)S(1)}) custom-call(bf16[480,384]{1,0:T(8,128)(2,1)S(1)} %get-tuple-element.24.normed_ref, bf16[384,384]{1,0:T(8,128)(2,1)S(1)} %copy-done.5, bf16[384,384]{1,0:T(8,128)(2,1)S(1)} %copy-done.6), custom_call_target="tpu_custom_call" | custom-call | flops 353894400 | bytes 368640 | tf_op jit(solution)/shard_map/attend_own/pallas_call | solution.py:283
  56.5 5.9 %collective-permute-done.11.refs_1_ = bf16[480,384]{1,0:T(8,128)(2,1)S(1)} collective-permute-done((bf16[480,384]{1,0:T(8,128)(2,1)S(1)}, bf16[480,384]{1,0:T(8,128)(2,1)S(1)}, u32[]{:S(2)}, u32[]{:S(2)}) %collective-permute-start.11) | collective-permute-done | bytes 368672 | tf_op jit(solution)/shard_map/ppermute | solution.py:175
  62.7 2.0 %collective-permute-start.8 = (bf16[240,384]{1,0:T(8,128)(2,1)S(1)}, bf16[240,384]{1,0:T(8,128)(2,1)S(1)}, u32[]{:S(2)}, u32[]{:S(2)}) collective-permute-start(bf16[240,384]{1,0:T(8,128)(2,1)S(1)} %slice.37), channel_id=1, source_target_pairs={{0,4},{1,5},{4,8},{5,9},{8,12},{9,13},{12,14},{13,15},{14,10},{15,... | collective-permute-start | bytes 552968 | tf_op jit(solution)/shard_map/ppermute | solution.py:175
  64.7 1.8 %attend_more.3 = (f32[480,128]{1,0:T(8,128)S(1)}, f32[480,128]{1,0:T(8,128)S(1)}, f32[480,384]{1,0:T(8,128)S(1)}) custom-call(bf16[480,384]{1,0:T(8,128)(2,1)S(1)} %get-tuple-element.25.query_ref, bf16[480,384]{1,0:T(8,128)(2,1)S(1)} %collective-permute-done.5.refs_0_, bf16[480,384]{1,0:T(8,128)(2,1)S(1)} %collective-permute-done.9.refs_1_, ...), custom_call_target="tpu_custom_call" | custom-call | flops 707788800 | bytes 737280 | tf_op jit(solution)/shard_map/attend_more/pallas_call | solution.py:291
  66.5 1.7 %attend_more.4 = (f32[480,128]{1,0:T(8,128)S(1)}, f32[480,128]{1,0:T(8,128)S(1)}, f32[480,384]{1,0:T(8,128)S(1)}) custom-call(bf16[480,384]{1,0:T(8,128)(2,1)S(1)} %get-tuple-element.25.query_ref, bf16[480,384]{1,0:T(8,128)(2,1)S(1)} %collective-permute-done.6.refs_0_, bf16[480,384]{1,0:T(8,128)(2,1)S(1)} %collective-permute-done.10.refs_1_, ...), custom_call_target="tpu_custom_call" | custom-call | flops 707788800 | bytes 737280 | tf_op jit(solution)/shard_map/attend_more/pallas_call | solution.py:291
  68.2 1.8 %attend_more.5 = (f32[480,128]{1,0:T(8,128)S(1)}, f32[480,128]{1,0:T(8,128)S(1)}, f32[480,384]{1,0:T(8,128)S(1)}) custom-call(bf16[480,384]{1,0:T(8,128)(2,1)S(1)} %get-tuple-element.25.query_ref, bf16[480,384]{1,0:T(8,128)(2,1)S(1)} %collective-permute-done.7.refs_0_, bf16[480,384]{1,0:T(8,128)(2,1)S(1)} %collective-permute-done.11.refs_1_, ...), custom_call_target="tpu_custom_call" | custom-call | flops 707788800 | bytes 737280 | tf_op jit(solution)/shard_map/attend_more/pallas_call | solution.py:291
  70.0 2.4 %attend_last.1 = bf16[480,384]{1,0:T(8,128)(2,1)} custom-call(bf16[480,384]{1,0:T(8,128)(2,1)S(1)} %get-tuple-element.25.query_ref, bf16[240,384]{1,0:T(8,128)(2,1)S(1)} %collective-permute-done.8.refs_0_, bf16[240,384]{1,0:T(8,128)(2,1)S(1)} %collective-permute-done.12.refs_1_, f32[480,128]{1,0:T(8,128)S(1)} %get-tuple-element.35.refs_2_, ...), custom_call_target="tpu_custom_call" | custom-call | flops 353894400 | bytes 368640 | tf_op jit(solution)/shard_map/attend_last/pallas_call | solution.py:299
  (33 shorter events, 3.5 us)
Async XLA Ops:
  0.0 17.5 %copy-start.2 = (bf16[3,160,384]{2,1,0:T(8,128)(2,1)S(1)}, bf16[3,160,384]{2,1,0:T(8,128)(2,1)}, u32[]{:S(2)}) copy-start(bf16[3,160,384]{2,1,0:T(8,128)(2,1)} %param.9) | copy-start | bytes 1105924
  0.0 24.5 %collective-permute-start.3 = (bf16[480,384]{1,0:T(8,128)(2,1)}, bf16[480,384]{1,0:T(8,128)(2,1)S(1)}, u32[]{:S(2)}, u32[]{:S(2)}) collective-permute-start(bf16[480,384]{1,0:T(8,128)(2,1)} %bitcast.13), channel_id=1, source_target_pairs={{14,0},{15,1},{0,2},{1,3},{2,4},{3,5},{4,6},{5,7},{6,8},{7,9},{8,1... | collective-permute-start | bytes 1105928 | tf_op jit(solution)/shard_map/ppermute | solution.py:175
  4.0 12.3 %collective-permute-start = (bf16[160,384]{1,0:T(8,128)(2,1)S(1)}, bf16[160,384]{1,0:T(8,128)(2,1)S(1)}, u32[]{:S(2)}, u32[]{:S(2)}) collective-permute-start(bf16[160,384]{1,0:T(8,128)(2,1)S(1)} %get-tuple-element.44), channel_id=1, source_target_pairs={{0,2},{1,3},{2,4},{3,5},{4,6},{5,7},{6,8},{7,9},{8,10},{9,11},{10,... | collective-permute-start | bytes 368648 | tf_op jit(solution)/shard_map/ppermute | solution.py:175
  7.4 10.0 %collective-permute-start.1 = (bf16[160,384]{1,0:T(8,128)(2,1)S(1)}, bf16[160,384]{1,0:T(8,128)(2,1)S(1)}, u32[]{:S(2)}, u32[]{:S(2)}) collective-permute-start(bf16[160,384]{1,0:T(8,128)(2,1)S(1)} %get-tuple-element.43), channel_id=1, source_target_pairs={{2,0},{3,1},{4,2},{5,3},{6,4},{7,5},{8,6},{9,7},{10,8},{11,9},{12,... | collective-permute-start | bytes 368648 | tf_op jit(solution)/shard_map/ppermute | solution.py:175
  9.7 14.7 %collective-permute-start.2 = (bf16[160,384]{1,0:T(8,128)(2,1)S(1)}, bf16[160,384]{1,0:T(8,128)(2,1)S(1)}, u32[]{:S(2)}, u32[]{:S(2)}) collective-permute-start(bf16[160,384]{1,0:T(8,128)(2,1)S(1)} %get-tuple-element.41), channel_id=1, source_target_pairs={{14,2},{15,3},{0,4},{1,5},{2,6},{3,7},{4,8},{5,9},{6,10},{7,11},{8... | collective-permute-start | bytes 368648 | tf_op jit(solution)/shard_map/ppermute | solution.py:175
  17.5 3.3 %copy-start = (bf16[3,3,3,384,384]{4,3,2,1,0:T(8,128)(2,1)S(1)}, bf16[3,3,3,384,384]{4,3,2,1,0:T(8,128)(2,1)}, u32[]{:S(2)}) copy-start(bf16[3,3,3,384,384]{4,3,2,1,0:T(8,128)(2,1)} %w_ref.5) | copy-start | bytes 23887876
  20.7 4.5 %copy-start.1 = (bf16[3,3,3,384,384]{4,3,2,1,0:T(8,128)(2,1)S(1)}, bf16[3,3,3,384,384]{4,3,2,1,0:T(8,128)(2,1)}, u32[]{:S(2)}) copy-start(bf16[3,3,3,384,384]{4,3,2,1,0:T(8,128)(2,1)} %w_ref.5) | copy-start | bytes 23887876
  24.5 0.7 copy-start.7
  24.7 3.7 %collective-permute-start.4 = (bf16[800,384]{1,0:T(8,128)(2,1)S(1)}, bf16[800,384]{1,0:T(8,128)(2,1)S(1)}, u32[]{:S(2)}, u32[]{:S(2)}) collective-permute-start(bf16[800,384]{1,0:T(8,128)(2,1)S(1)} %get-tuple-element.40), channel_id=1, source_target_pairs={{0,1},{1,0},{2,3},{3,2},{4,5},{5,4},{6,7},{7,6},{8,9},{9,8},{10,11... | collective-permute-start | bytes 1843208 | tf_op jit(solution)/shard_map/ppermute | solution.py:175
  28.4 26.8 %copy-start.5 = (bf16[384,384]{1,0:T(8,128)(2,1)S(1)}, bf16[384,384]{1,0:T(8,128)(2,1)}, u32[]{:S(2)}) copy-start(bf16[384,384]{1,0:T(8,128)(2,1)} %wq_ref.1) | copy-start | bytes 884740
  28.4 26.8 %copy-start.6 = (bf16[384,384]{1,0:T(8,128)(2,1)S(1)}, bf16[384,384]{1,0:T(8,128)(2,1)}, u32[]{:S(2)}) copy-start(bf16[384,384]{1,0:T(8,128)(2,1)} %wk_ref.1) | copy-start | bytes 884740
  31.8 11.2 %collective-permute-start.9 = (bf16[480,384]{1,0:T(8,128)(2,1)S(1)}, bf16[480,384]{1,0:T(8,128)(2,1)S(1)}, u32[]{:S(2)}, u32[]{:S(2)}) collective-permute-start(bf16[480,384]{1,0:T(8,128)(2,1)S(1)} %get-tuple-element.24.normed_ref), channel_id=1, source_target_pairs={{4,0},{5,1},{8,4},{9,5},{12,8},{13,9},{14,12},{15,13},{10,14},{11,... | collective-permute-start | bytes 1105928 | tf_op jit(solution)/shard_map/ppermute | solution.py:175
  33.2 10.6 %collective-permute-start.5 = (bf16[480,384]{1,0:T(8,128)(2,1)S(1)}, bf16[480,384]{1,0:T(8,128)(2,1)S(1)}, u32[]{:S(2)}, u32[]{:S(2)}) collective-permute-start(bf16[480,384]{1,0:T(8,128)(2,1)S(1)} %get-tuple-element.24.normed_ref), channel_id=1, source_target_pairs={{0,4},{1,5},{4,8},{5,9},{8,12},{9,13},{12,14},{13,15},{14,10},{15,... | collective-permute-start | bytes 1105928 | tf_op jit(solution)/shard_map/ppermute | solution.py:175
  43.1 10.1 %collective-permute-start.10 = (bf16[480,384]{1,0:T(8,128)(2,1)S(1)}, bf16[480,384]{1,0:T(8,128)(2,1)S(1)}, u32[]{:S(2)}, u32[]{:S(2)}) collective-permute-start(bf16[480,384]{1,0:T(8,128)(2,1)S(1)} %collective-permute-done.9.refs_1_), channel_id=1, source_target_pairs={{4,0},{5,1},{8,4},{9,5},{12,8},{13,9},{14,12},{15,13},{10,14},{11,... | collective-permute-start | bytes 1105928 | tf_op jit(solution)/shard_map/ppermute | solution.py:175
  43.9 9.8 %collective-permute-start.6 = (bf16[480,384]{1,0:T(8,128)(2,1)S(1)}, bf16[480,384]{1,0:T(8,128)(2,1)S(1)}, u32[]{:S(2)}, u32[]{:S(2)}) collective-permute-start(bf16[480,384]{1,0:T(8,128)(2,1)S(1)} %collective-permute-done.5.refs_0_), channel_id=1, source_target_pairs={{0,4},{1,5},{4,8},{5,9},{8,12},{9,13},{12,14},{13,15},{14,10},{15,... | collective-permute-start | bytes 1105928 | tf_op jit(solution)/shard_map/ppermute | solution.py:175
  53.1 9.2 %collective-permute-start.11 = (bf16[480,384]{1,0:T(8,128)(2,1)S(1)}, bf16[480,384]{1,0:T(8,128)(2,1)S(1)}, u32[]{:S(2)}, u32[]{:S(2)}) collective-permute-start(bf16[480,384]{1,0:T(8,128)(2,1)S(1)} %collective-permute-done.10.refs_1_), channel_id=1, source_target_pairs={{4,0},{5,1},{8,4},{9,5},{12,8},{13,9},{14,12},{15,13},{10,14},{11,... | collective-permute-start | bytes 1105928 | tf_op jit(solution)/shard_map/ppermute | solution.py:175
  53.6 9.1 %collective-permute-start.7 = (bf16[480,384]{1,0:T(8,128)(2,1)S(1)}, bf16[480,384]{1,0:T(8,128)(2,1)S(1)}, u32[]{:S(2)}, u32[]{:S(2)}) collective-permute-start(bf16[480,384]{1,0:T(8,128)(2,1)S(1)} %collective-permute-done.6.refs_0_), channel_id=1, source_target_pairs={{0,4},{1,5},{4,8},{5,9},{8,12},{9,13},{12,14},{13,15},{14,10},{15,... | collective-permute-start | bytes 1105928 | tf_op jit(solution)/shard_map/ppermute | solution.py:175
  62.3 7.6 %collective-permute-start.12 = (bf16[240,384]{1,0:T(8,128)(2,1)S(1)}, bf16[240,384]{1,0:T(8,128)(2,1)S(1)}, u32[]{:S(2)}, u32[]{:S(2)}) collective-permute-start(bf16[240,384]{1,0:T(8,128)(2,1)S(1)} %slice.38), channel_id=1, source_target_pairs={{4,0},{5,1},{8,4},{9,5},{12,8},{13,9},{14,12},{15,13},{10,14},{11,... | collective-permute-start | bytes 552968 | tf_op jit(solution)/shard_map/ppermute | solution.py:175
  62.7 7.3 %collective-permute-start.8 = (bf16[240,384]{1,0:T(8,128)(2,1)S(1)}, bf16[240,384]{1,0:T(8,128)(2,1)S(1)}, u32[]{:S(2)}, u32[]{:S(2)}) collective-permute-start(bf16[240,384]{1,0:T(8,128)(2,1)S(1)} %slice.37), channel_id=1, source_target_pairs={{0,4},{1,5},{4,8},{5,9},{8,12},{9,13},{12,14},{13,15},{14,10},{15,... | collective-permute-start | bytes 552968 | tf_op jit(solution)/shard_map/ppermute | solution.py:175
  68.2 1.8 %copy-start.3 = (bf16[384,384]{1,0:T(8,128)(2,1)S(1)}, bf16[384,384]{1,0:T(8,128)(2,1)}, u32[]{:S(2)}) copy-start(bf16[384,384]{1,0:T(8,128)(2,1)} %refs_6_.1) | copy-start | bytes 884740
  68.2 1.8 %copy-start.4 = (bf16[384,384]{1,0:T(8,128)(2,1)S(1)}, bf16[384,384]{1,0:T(8,128)(2,1)}, u32[]{:S(2)}) copy-start(bf16[384,384]{1,0:T(8,128)(2,1)} %refs_7_.1) | copy-start | bytes 884740
